TPU v7x, 32 devices: a whole 2x2x4 slice. The times are simulated.
32 devices in a mesh: tm: 8 (over z, y), tensor: 4 (over x, core).
Axes of the slice: x: 2, y: 2, z: 4, core: 2. Of those that a mesh axis runs over, the one named last changes fastest.
Arguments:
- frames_in: bfloat16 [8, 1024, 768], P('tm'), may hold values from -16 to 16
- norm_gain: float32 [768], replicated, may hold values from 0.1 to 1.9
- w_qkv: bfloat16 [768, 3, 768], P(None, None, 'tensor'), may hold values from -0.21650635 to 0.21650635
- w_out: bfloat16 [768, 768], P('tensor'), may hold values from -0.21875 to 0.21875
- keep_runs: int32 [8, 16, 2], replicated, may hold values from 0 to 1023, as said below
- out_cotangent: bfloat16 [8, 1024, 768], P('tm'), may hold values from -6 to 6
Outputs:
- block_out: bfloat16 [8, 1024, 768], P('tm', None, 'tensor')
- grad_in: bfloat16 [8, 1024, 768], P('tm', None, 'tensor')
- grad_qkv: bfloat16 [768, 3, 768], P('tm', None, 'tensor')
- grad_proj: bfloat16 [768, 768], P('tensor', 'tm')
- grad_gain: float32 [768], P('tensor')
Inputs may be any that keep to these rules, and one draw needn't show every extreme that they name: keep_runs[t, r] = (first, length) is the r-th run of kept positions of frame t; the 16 runs of a frame are disjoint, in rising order, and lie within the frame's 1024 positions.
All inputs are finite; a program needn't handle non-finite values.
Results may differ from a plain program's by a relative error of at most 0.034.
Values may be sent and summed in bfloat16 or wider, within the bound.
No kernel may reach another device: no remote copies, remote signals or barrier semaphores. Data moves between devices by JAX's collectives and lax.ppermute only.
A program may use at most 128 MiB of HBM per device.

v0:
```python
import jax
import jax.numpy as jnp
from jax import lax
from jax.sharding import PartitionSpec as P

D = 768
H = 12
epsilon = 1e-05


def kept_table(keep_runs, first_place, place_count):
    places = first_place + jnp.arange(place_count, dtype=jnp.int32)
    starts = keep_runs[:, :, 0:1]
    lengths = keep_runs[:, :, 1:2]
    inside = (places[None, None, :] >= starts) & (places[None, None, :] < starts + lengths)
    return jnp.sum(inside.astype(jnp.int32), axis=1)


def normalize(frames_in):
    frames_float = frames_in.astype(jnp.float32)
    centre = jnp.mean(frames_float, axis=-1, keepdims=True)
    shifted = frames_float - centre
    spread = jnp.mean(shifted * shifted, axis=-1, keepdims=True)
    inverse_spread = lax.rsqrt(spread + epsilon)
    return (frames_float, shifted * inverse_spread, inverse_spread)


def attend(packed, kept_mask):
    frames, places, row_width = packed.shape
    head_width = D // H
    pieces = packed.reshape(frames, places, 3, row_width // (3 * head_width), head_width)
    scores = jnp.einsum(
        "tphd,uphd->phtu", pieces[:, :, 0], pieces[:, :, 1], preferred_element_type=jnp.float32
    )
    scores = scores * head_width ** (-0.5)
    allowed = jnp.transpose(kept_mask)[:, None, None, :] > 0
    scores = jnp.where(allowed, scores, -1000000000.0)
    row_max = jnp.max(scores, axis=-1, keepdims=True)
    exponent = jnp.exp(scores - row_max)
    weights = (exponent / jnp.sum(exponent, axis=-1, keepdims=True)).astype(jnp.bfloat16)
    mixed_rows = jnp.einsum(
        "phtu,uphd->tphd", weights, pieces[:, :, 2], preferred_element_type=jnp.float32
    )
    mixed_rows = jnp.where(kept_mask[:, :, None, None] > 0, mixed_rows, 0.0)
    return mixed_rows.astype(jnp.bfloat16).reshape(frames, places, row_width // 3)


def project(rows_in, weight):
    leading = rows_in.shape[:-1]
    flat = jnp.dot(
        rows_in.reshape(-1, rows_in.shape[-1]), weight, preferred_element_type=jnp.float32
    )
    return flat.astype(jnp.bfloat16).reshape(leading + (weight.shape[1],))


def contract_rows(left, right):
    return lax.dot_general(
        left.reshape(-1, left.shape[-1]),
        right.reshape(-1, right.shape[-1]),
        (((0,), (0,)), ((), ())),
        preferred_element_type=jnp.float32,
    )


def back_project(cotangent, weight):
    leading = cotangent.shape[:-1]
    flat = lax.dot_general(
        cotangent.reshape(-1, cotangent.shape[-1]),
        weight,
        (((1,), (1,)), ((), ())),
        preferred_element_type=jnp.float32,
    )
    return flat.reshape(leading + (weight.shape[0],))


def body(frames_in, norm_gain, w_qkv, w_out, keep_runs, out_cotangent):
    frames_here, place_total, row_width = frames_in.shape
    places_here = place_total // lax.axis_size("tm")
    width_share = row_width // lax.axis_size("tensor")
    share_start = lax.axis_index("tensor") * width_share
    channels = w_qkv.shape[2]
    w_flat = w_qkv.reshape(row_width, 3 * channels)
    kept_mask = kept_table(keep_runs, lax.axis_index("tm") * places_here, places_here)
    frames_float, standard, inverse_spread = normalize(frames_in)
    normed = (standard * norm_gain).astype(jnp.bfloat16)
    packed = project(normed, w_flat)
    packed_places = lax.all_to_all(packed, "tm", split_axis=1, concat_axis=0, tiled=True)

    def attend_here(packed_arg):
        return attend(packed_arg, kept_mask)

    mixed_places, attend_back = jax.vjp(attend_here, packed_places)
    mixed_frames = lax.all_to_all(mixed_places, "tm", split_axis=0, concat_axis=1, tiled=True)
    branch = jnp.dot(mixed_frames.reshape(-1, channels), w_out, preferred_element_type=jnp.float32)
    branch = branch.reshape(frames_here, place_total, row_width)
    branch_share = lax.psum_scatter(
        branch.astype(jnp.bfloat16), "tensor", scatter_dimension=2, tiled=True
    ).astype(jnp.float32)
    residual_share = lax.dynamic_slice_in_dim(frames_float, share_start, width_share, 2)
    block_out = (residual_share + branch_share).astype(jnp.bfloat16)
    proj_part = contract_rows(mixed_frames, out_cotangent)
    grad_proj = lax.psum_scatter(proj_part, "tm", scatter_dimension=1, tiled=True).astype(
        jnp.bfloat16
    )
    mixed_cot = back_project(out_cotangent, w_out).astype(jnp.bfloat16)
    mixed_cot_places = lax.all_to_all(mixed_cot, "tm", split_axis=1, concat_axis=0, tiled=True)
    packed_cot_places = attend_back(mixed_cot_places)[0]
    gain_share = lax.dynamic_slice_in_dim(norm_gain, share_start, width_share, 0)
    standard_share = lax.dynamic_slice_in_dim(standard, share_start, width_share, 2)
    packed_cot = lax.all_to_all(packed_cot_places, "tm", split_axis=0, concat_axis=1, tiled=True)
    qkv_part = contract_rows(normed, packed_cot)
    normed_part = back_project(packed_cot, w_flat)
    whole_cot = lax.psum(normed_part.astype(jnp.bfloat16), "tensor").astype(jnp.float32)
    whole_cot = lax.optimization_barrier(whole_cot.astype(jnp.bfloat16)).astype(jnp.float32)
    scaled_whole = whole_cot * norm_gain
    mean_plain = jnp.mean(scaled_whole, axis=-1, keepdims=True)
    mean_cross = jnp.mean(scaled_whole * standard, axis=-1, keepdims=True)
    cot_share = lax.dynamic_slice_in_dim(whole_cot, share_start, width_share, 2)
    scaled_share = cot_share * gain_share
    through = inverse_spread * (scaled_share - mean_plain - standard_share * mean_cross)
    gain_part = jnp.sum(cot_share * standard_share, axis=(0, 1))
    cot_share_out = lax.dynamic_slice_in_dim(out_cotangent, share_start, width_share, 2).astype(
        jnp.float32
    )
    grad_in = (cot_share_out + through).astype(jnp.bfloat16)
    grad_qkv = lax.psum_scatter(
        qkv_part.reshape(row_width, 3, channels), "tm", scatter_dimension=0, tiled=True
    ).astype(jnp.bfloat16)
    grad_gain = lax.psum(gain_part, "tm")
    return (block_out, grad_in, grad_qkv, grad_proj, grad_gain)


def solution(mesh):
    in_specs = (
        P("tm", None, None),
        P(),
        P(None, None, "tensor"),
        P("tensor", None),
        P(),
        P("tm", None, None),
    )
    out_specs = (
        P("tm", None, "tensor"),
        P("tm", None, "tensor"),
        P("tm", None, "tensor"),
        P("tensor", "tm"),
        P("tensor"),
    )
    return jax.shard_map(body, mesh=mesh, in_specs=in_specs, out_specs=out_specs, check_vma=False)
```

profile of v0, /device:TPU:0, one launch (start us, length us, event | category | flops | bytes accessed | tf_op | source)
XLA Modules:
  0.0 338.7 jit_solution(6467486779215469923)
XLA Ops:
  8.0 2.2 fusion.29
  10.2 0.8 copy.115
  11.0 0.5 broadcast.97
  11.6 4.9 %reduce.4 = bf16[1024,192]{1,0:T(8,128)(2,1)} reduce(bf16[1024,1,192]{2,1,0:T(2,128)(2,1)S(1)} %bitcast.147, bf16[]{:T(256)} %broadcast.97), dimensions={1}, to_apply=%bitcast.110.reduce_sub_computation | reduce | bytes 786434
  16.5 2.4 reshape.160
  18.9 7.7 %all-to-all-start.2 = ((bf16[8,2,12288]{2,1,0:T(2,128)(2,1)}), bf16[8,2,12288]{2,1,0:T(2,128)(2,1)S(1)}, u32[]{:S(2)}, u32[]{:S(2)}) async-start(bf16[8,2,12288]{2,1,0:T(2,128)(2,1)} %reshape.160), calls=%async_computation.2 | async-start | bytes 786432 | tf_op jit(solution)/shard_map/all_to_all | solution.py:106
  27.0 0.6 multiply_reduce_fusion.1
  27.6 2.3 fusion.17
  29.9 6.2 %copy.106 = bf16[1,1024,576]{2,0,1:T(2,128)(2,1)} copy(bf16[1,1024,576]{1,2,0:T(8,128)(2,1)} %fusion.17) | data formatting | bytes 2359296 | tf_op jit(solution)/shard_map/reshape | solution.py:53
  36.1 11.0 %reduce.5 = bf16[1024,576]{1,0:T(8,128)(2,1)} reduce(bf16[1024,1,576]{2,1,0:T(2,128)(2,1)} %bitcast.141, bf16[]{:T(256)} %broadcast.97), dimensions={1}, to_apply=%bitcast.108.reduce_sub_computation | reduce | bytes 2359298
  47.1 4.4 %reshape.158 = bf16[8,2,36864]{2,1,0:T(2,128)(2,1)} reshape(bf16[1024,576]{1,0:T(8,128)(2,1)} %reduce.5) | data formatting | bytes 2359296
  51.5 17.1 %all-to-all-start = ((bf16[8,2,36864]{2,1,0:T(2,128)(2,1)}), bf16[8,2,36864]{2,1,0:T(2,128)(2,1)}, u32[]{:S(2)}, u32[]{:S(2)}) async-start(bf16[8,2,36864]{2,1,0:T(2,128)(2,1)} %reshape.158), calls=%async_computation | async-start | bytes 2359296 | tf_op jit(solution)/shard_map/all_to_all | solution.py:87
  69.0 2.4 reshape.161
  71.4 1.7 copy.116
  73.1 1.8 copy.143
  74.9 22.0 %all-to-all-done = bf16[8,2,36864]{2,1,0:T(2,128)(2,1)} async-done(((bf16[8,2,36864]{2,1,0:T(2,128)(2,1)}), bf16[8,2,36864]{2,1,0:T(2,128)(2,1)}, u32[]{:S(2)}, u32[]{:S(2)}) %all-to-all-start) | async-done | bytes 1179680 | tf_op jit(solution)/shard_map/all_to_all | solution.py:87
  96.9 6.5 %reshape.159 = bf16[1024,1,576]{2,1,0:T(2,128)(2,1)} reshape(bf16[8,2,36864]{2,1,0:T(2,128)(2,1)} %all-to-all-done) | data formatting | bytes 2359296
  103.4 6.0 %copy.107 = bf16[1,1024,576]{1,2,0:T(8,128)(2,1)} copy(bf16[1,1024,576]{2,0,1:T(2,128)(2,1)} %bitcast.142) | data formatting | bytes 2359296 | tf_op jit(solution)/shard_map/all_to_all | solution.py:87
  109.4 1.6 copy.142
  111.0 1.0 fusion.60
  112.0 1.6 copy.138
  113.6 2.7 copy.137
  116.3 2.4 copy.139
  118.7 2.0 fusion.62
  120.8 0.7 fusion.32
  121.5 0.8 multiply_divide_fusion
  122.5 1.6 fusion.39
  124.0 2.3 copy.113
  126.3 2.1 fusion.41
  128.4 3.5 %all-to-all-start.1 = ((bf16[8,128,192]{1,2,0:T(8,128)(2,1)}), bf16[8,128,192]{1,2,0:T(8,128)(2,1)S(1)}, u32[]{:S(2)}, u32[]{:S(2)}) async-start(bf16[8,128,192]{1,2,0:T(8,128)(2,1)} %bitcast.149), calls=%async_computation.1 | async-start | bytes 786432 | tf_op jit(solution)/shard_map/all_to_all | solution.py:93
  131.9 2.2 copy.118
  134.1 3.7 %convert_reduce_fusion.1 = (f32[128,3,8]{2,1,0:T(4,128)S(1)}, pred[128,3,8,8]{2,3,1,0:T(8,128)(4,1)S(1)}, f32[128,3,8]{2,1,0:T(4,128)S(1)}, bf16[128,3,8,8]{2,3,1,0:T(8,128)(2,1)S(1)}) fusion(f32[128,3,8,8]{2,3,1,0:T(8,128)} %copy-done.2, f32[128,3,8]{2,1,0:T(4,128)S(1)} %get-tuple-element.57, f32[128,3,8]{2,1,0:T(4,128)} %multiply_divide_fusion, ...), kind=kOutput, calls=%fused_computation.25 | convolution fusion | flops 3336192 | bytes 1007616 | tf_op jit(solution)/shard_map/transpose(jvp(phtu,uphd->tphd))/dot_general | solution.py:41
  137.9 1.0 fusion.58
  139.0 1.0 fusion.22
  140.2 0.7 fusion.21
  140.8 0.5 copy-done.12
  141.3 0.6 fusion.20
  141.9 2.0 pad_add_fusion
  143.9 4.0 %copy.121 = bf16[8,128,3,3,64]{1,4,3,2,0:T(8,128)(2,1)} copy(bf16[8,128,3,3,64]{4,0,3,1,2:T(8,128)(2,1)} %pad_add_fusion) | data formatting | bytes 2359296 | tf_op jit(solution)/shard_map/transpose(jvp())/add_any | solution.py:33
  147.9 6.0 %all-to-all-start.3 = ((bf16[8,128,576]{1,2,0:T(8,128)(2,1)}), bf16[8,128,576]{1,2,0:T(8,128)(2,1)}, u32[]{:S(2)}, u32[]{:S(2)}) async-start(bf16[8,128,576]{1,2,0:T(8,128)(2,1)} %bitcast.144), calls=%async_computation.3 | async-start | bytes 2359296 | tf_op jit(solution)/shard_map/all_to_all | solution.py:110
  153.9 3.0 fusion.23
  157.0 28.6 %all-to-all-done.3 = bf16[8,128,576]{1,2,0:T(8,128)(2,1)} async-done(((bf16[8,128,576]{1,2,0:T(8,128)(2,1)}), bf16[8,128,576]{1,2,0:T(8,128)(2,1)}, u32[]{:S(2)}, u32[]{:S(2)}) %all-to-all-start.3) | async-done | bytes 1179680 | tf_op jit(solution)/shard_map/all_to_all | solution.py:110
  185.6 3.9 %fusion.16 = bf16[1,1024,768]{2,1,0:T(8,128)(2,1)} fusion(bf16[768,576]{0,1:T(8,128)(2,1)S(1)} %bitcast.139, bf16[8,128,576]{1,2,0:T(8,128)(2,1)} %all-to-all-done.3), kind=kOutput, calls=%fused_computation.31 | convolution fusion | flops 906756096 | bytes 3637248 | tf_op jit(solution)/shard_map/dot_general | solution.py:67
  189.6 0.9 copy-done.10
  190.5 1.8 fusion.15
  192.2 8.5 %copy.130 = bf16[1,1024,768]{1,0,2:T(2,128)(2,1)} copy(bf16[1,1024,768]{2,1,0:T(8,128)(2,1)} %fusion.15) | data formatting | bytes 3145728
  200.7 3.7 %copy.158 = bf16[768,1,1024]{2,0,1:T(8,128)(2,1)} copy(bf16[768,1,1024]{2,1,0:T(2,128)(2,1)} %bitcast.140) | data formatting | bytes 3145728
  204.7 1.4 copy_bitcast_fusion.1
  206.1 3.3 fusion.4
  209.4 1.9 convert_element_type.92
  211.4 15.4 %reduce-scatter.12.cloned.1.call-done = f32[96,192]{1,0:T(8,128)} async-done(((f32[768,192]{1,0:T(8,128)}), f32[96,192]{1,0:T(8,128)}) %reduce-scatter.12.cloned.1.call-update) | async-done | bytes 73744
  226.8 1.6 copy.133
  228.4 3.5 %all-reduce.5.cloned.1.call-done = bf16[1,1024,768]{2,1,0:T(8,128)(2,1)} async-done(((bf16[1,1024,768]{2,1,0:T(8,128)(2,1)}), bf16[1,1024,768]{2,1,0:T(8,128)(2,1)}) %all-reduce.5.cloned.1.call-update) | async-done | bytes 1572880 | tf_op jit(solution)/shard_map/psum | solution.py:113
  232.0 1.8 convert_element_type.118
  233.9 1.2 multiply_reduce_fusion.2
  235.1 2.5 multiply_reduce_fusion.3
  237.6 0.9 copy.125
  238.5 21.8 %psum.15 = f32[192]{0:T(256)} all-reduce(f32[192]{0:T(256)S(1)} %get-tuple-element.46), channel_id=1, replica_groups=mesh['tm'=8,'tensor'=4] {'tm'}, use_global_device_ids=true, to_apply=%region_15.16 | all-reduce | flops 192 | bytes 1536 | tf_op jit(solution)/shard_map/psum | solution.py:129
  260.4 1.4 reshape_bitcast_fusion
  261.8 1.1 copy.131
  262.9 1.8 add_convert_fusion.1
  264.7 0.9 copy.124
  265.6 64.1 %reduce-scatter.8.cloned.1.call-done = f32[96,3,192]{2,0,1:T(8,128)} async-done(((f32[768,3,192]{2,0,1:T(8,128)}), f32[96,3,192]{2,0,1:T(8,128)}) %reduce-scatter.8.cloned.1.call-update) | async-done | bytes 221200 | tf_op jit(solution)/shard_map/reduce_scatter | solution.py:126
  329.7 1.6 convert_element_type.120
  (53 shorter events, 1.8 us)
Async XLA Ops:
  8.0 19.6 %copy-start = (bf16[768,3,192]{0,2,1:T(8,128)(2,1)S(1)}, bf16[768,3,192]{0,2,1:T(8,128)(2,1)}, u32[]{:S(2)}) copy-start(bf16[768,3,192]{0,2,1:T(8,128)(2,1)} %param.8) | copy-start | bytes 2654212
  11.6 15.1 %copy-start.1 = (bf16[1,1024,768]{2,1,0:T(8,128)(2,1)S(1)}, bf16[1,1024,768]{2,1,0:T(8,128)(2,1)}, u32[]{:S(2)}) copy-start(bf16[1,1024,768]{2,1,0:T(8,128)(2,1)} %param.6) | copy-start | bytes 4718596
  18.9 32.6 %all-to-all-start.2 = ((bf16[8,2,12288]{2,1,0:T(2,128)(2,1)}), bf16[8,2,12288]{2,1,0:T(2,128)(2,1)S(1)}, u32[]{:S(2)}, u32[]{:S(2)}) async-start(bf16[8,2,12288]{2,1,0:T(2,128)(2,1)} %reshape.160), calls=%async_computation.2 | async-start | bytes 786432 | tf_op jit(solution)/shard_map/all_to_all | solution.py:106
  26.7 0.9 copy-start.14
  51.5 17.2 %copy-start.13 = (s32[8,16,2]{1,2,0:T(2,128)S(1)}, s32[8,16,2]{1,2,0:T(2,128)}, u32[]{:S(2)}) copy-start(s32[8,16,2]{1,2,0:T(2,128)} %param.10) | copy-start | bytes 3076
  51.5 17.5 %copy-start.8 = (bf16[8,2,12288]{2,1,0:T(2,128)(2,1)}, bf16[8,2,12288]{2,1,0:T(2,128)(2,1)S(1)}, u32[]{:S(2)}) copy-start(bf16[8,2,12288]{2,1,0:T(2,128)(2,1)S(1)} %all-to-all-done.2) | copy-start | bytes 1179652
  51.5 45.4 %all-to-all-start = ((bf16[8,2,36864]{2,1,0:T(2,128)(2,1)}), bf16[8,2,36864]{2,1,0:T(2,128)(2,1)}, u32[]{:S(2)}, u32[]{:S(2)}) async-start(bf16[8,2,36864]{2,1,0:T(2,128)(2,1)} %reshape.158), calls=%async_computation | async-start | bytes 2359296 | tf_op jit(solution)/shard_map/all_to_all | solution.py:87
  113.6 7.1 %copy-start.5 = (bf16[8,128,1,3,64]{4,0,3,1,2:T(8,128)(2,1)}, bf16[8,128,1,3,64]{4,0,3,1,2:T(8,128)(2,1)S(1)}, u32[]{:S(2)}) copy-start(bf16[8,128,1,3,64]{4,0,3,1,2:T(8,128)(2,1)S(1)} %copy.138) | copy-start | bytes 1179652
  120.7 1.5 copy-start.2
  120.7 1.7 copy-start.11
  122.4 3.9 %copy-start.9 = (bf16[24,8,8,128]{3,2,1,0:T(8,128)(2,1)S(1)}, bf16[24,8,8,128]{3,2,1,0:T(8,128)(2,1)}, u32[]{:S(2)}) copy-start(bf16[24,8,8,128]{3,2,1,0:T(8,128)(2,1)} %copy.143) | copy-start | bytes 1179652
  128.4 19.5 %all-to-all-start.1 = ((bf16[8,128,192]{1,2,0:T(8,128)(2,1)}), bf16[8,128,192]{1,2,0:T(8,128)(2,1)S(1)}, u32[]{:S(2)}, u32[]{:S(2)}) async-start(bf16[8,128,192]{1,2,0:T(8,128)(2,1)} %bitcast.149), calls=%async_computation.1 | async-start | bytes 786432 | tf_op jit(solution)/shard_map/all_to_all | solution.py:93
  134.1 3.8 %copy-start.3 = (f32[128,3,8,8]{2,3,1,0:T(8,128)S(1)}, f32[128,3,8,8]{2,3,1,0:T(8,128)}, u32[]{:S(2)}) copy-start(f32[128,3,8,8]{2,3,1,0:T(8,128)} %copy-done.2) | copy-start | bytes 294916
  137.9 1.1 copy-start.7
  139.0 1.1 copy-start.6
  140.2 1.1 copy-start.12
  147.9 37.7 %all-to-all-start.3 = ((bf16[8,128,576]{1,2,0:T(8,128)(2,1)}), bf16[8,128,576]{1,2,0:T(8,128)(2,1)}, u32[]{:S(2)}, u32[]{:S(2)}) async-start(bf16[8,128,576]{1,2,0:T(8,128)(2,1)} %bitcast.144), calls=%async_computation.3 | async-start | bytes 2359296 | tf_op jit(solution)/shard_map/all_to_all | solution.py:110
  153.9 72.9 %reduce-scatter.12.cloned.1.call-start = ((), (), s32[]{:S(2)}) async-start(), calls=%async_computation.10 | async-start | bytes 884736
  157.0 75.0 %all-reduce.5.cloned.1.call-start = ((), (), s32[]{:S(2)}) async-start(), calls=%async_computation.7 | async-start | bytes 3145728 | tf_op jit(solution)/shard_map/psum | solution.py:113
  189.5 1.0 copy-start.10
  189.5 70.8 %reduce-scatter.10.cloned.1.call-start = ((), (), s32[]{:S(2)}) async-start(), calls=%async_computation.9 | async-start | bytes 1966080
  204.4 125.2 %reduce-scatter.8.cloned.1.call-start = ((), (), s32[]{:S(2)}) async-start(), calls=%async_computation.8 | async-start | bytes 2654208 | tf_op jit(solution)/shard_map/reduce_scatter | solution.py:126
  232.0 2.0 copy-start.4
Sparse Core Ops, SparseCore 0:
  158.0 68.7 reduce-scatter.11
  229.4 27.0 reduce-scatter.9
  260.0 69.6 reduce-scatter.7
Sparse Core Ops, SparseCore 1:
  189.6 42.3 all-reduce.4
where the time goes:
time: 345 us; the launch traced here: 339 us
  waiting for transfers between devices  134 us (39%)
  local copies, waits for them, and re-layouts  72.4 us (21%)
  starting transfers between devices  34.6 us (10%)
  other arithmetic  34.4 us (10%)
  matrix products  25.9 us (8%)
  blocking collectives  21.8 us (6%)
  between operations  15.8 us (5%)
    reduce_scatter x1, waiting for transfers between devices, body(): lax.psum_scatter(qkv_part.reshape(row_width, 3, channels), 'tm', scatter_...  64.1 us
    unnamed x47, local copies, waits for them, and re-layouts  46.5 us
    all_to_all x1, waiting for transfers between devices, body(): lax.all_to_all(packed_cot_places, 'tm', split_axis=0, concat_axis=1, tile...  28.6 us
    all_to_all x1, waiting for transfers between devices, body(): lax.all_to_all(packed, 'tm', split_axis=1, concat_axis=0, tiled=True)  22 us
    psum x1, blocking collectives, body(): grad_gain = lax.psum(gain_part, 'tm')  21.8 us
    all_to_all x1, starting transfers between devices, body(): lax.all_to_all(packed, 'tm', split_axis=1, concat_axis=0, tiled=True)  17.1 us
    unnamed x2, other arithmetic  16 us
    unnamed x6, waiting for transfers between devices  15.5 us
  transfers between devices with their start and end apart: 8, of which 5 were waited for; matrix products, arithmetic and copies ran while one was open for 26% of the time, Pallas kernels for 0%

commit v1 on v0

--- a/solution.py
+++ b/solution.py
@@ -126,7 +126,10 @@
     grad_qkv = lax.psum_scatter(
         qkv_part.reshape(row_width, 3, channels), "tm", scatter_dimension=0, tiled=True
     ).astype(jnp.bfloat16)
-    grad_gain = lax.psum(gain_part, "tm")
+    count, grad_gain = (lax.axis_size("tm"), gain_part)
+    for far in [1 << k for k in range(count.bit_length() - 1)]:
+        swap = [(i, i ^ far) for i in range(count)]
+        grad_gain = grad_gain + lax.ppermute(grad_gain, "tm", swap)
     return (block_out, grad_in, grad_qkv, grad_proj, grad_gain)
 
 

time: 345 us -> 364 us (1.055)
  waiting for transfers between devices: 134 us -> 154 us
  starting transfers between devices: 34.6 us -> 23.1 us
  blocking collectives: 21.8 us -> 32.7 us
    all_to_all x0 -> x1, blocking collectives: none -> 32.7 us  [body(): lax.all_to_all(packed_cot_places, 'tm', split_axis=0, concat_axis=1, tile...]
    all_to_all x1 -> x0, waiting for transfers between devices: 28.6 us -> none  [body(): lax.all_to_all(packed_cot_places, 'tm', split_axis=0, concat_axis=1, tile...]
    unnamed x6, waiting for transfers between devices: 15.5 us -> 37.7 us
    psum x1 -> x0, blocking collectives: 21.8 us -> none  [body(): grad_gain = lax.psum(gain_part, 'tm')]
    psum x1, waiting for transfers between devices: 3.54 us -> 15.2 us  [body(): lax.psum(normed_part.astype(jnp.bfloat16), 'tensor').astype(jnp.float32)]
    all_to_all x1, starting transfers between devices: 17.1 us -> 6.23 us  [body(): lax.all_to_all(packed, 'tm', split_axis=1, concat_axis=0, tiled=True)]
    all_to_all x1, waiting for transfers between devices: 0.01 us -> 7.05 us  [body(): lax.all_to_all(mixed_places, 'tm', split_axis=0, concat_axis=1, tiled=True)]
    all_to_all x1 -> x0, starting transfers between devices: 5.97 us -> none  [body(): lax.all_to_all(packed_cot_places, 'tm', split_axis=0, concat_axis=1, tile...]
  transfers between devices with their start and end apart: 8 -> 10, of which waited for: 5 -> 8; matrix products, arithmetic and copies ran while one was open for 26% -> 20% of each run, Pallas kernels for 0% -> 0%
where the time goes in v1:
time: 364 us; the launch traced here: 358 us
  waiting for transfers between devices  154 us (42%)
  local copies, waits for them, and re-layouts  71.2 us (20%)
  other arithmetic  34.9 us (10%)
  blocking collectives  32.7 us (9%)
  matrix products  25.9 us (7%)
  starting transfers between devices  23.1 us (6%)
  between operations  16.3 us (4%)
    reduce_scatter x1, waiting for transfers between devices, body(): lax.psum_scatter(qkv_part.reshape(row_width, 3, channels), 'tm', scatter_...  67.9 us
    unnamed x49, local copies, waits for them, and re-layouts  45 us
    unnamed x6, waiting for transfers between devices  37.7 us
    all_to_all x1, blocking collectives, body(): lax.all_to_all(packed_cot_places, 'tm', split_axis=0, concat_axis=1, tile...  32.7 us
    all_to_all x1, waiting for transfers between devices, body(): lax.all_to_all(packed, 'tm', split_axis=1, concat_axis=0, tiled=True)  22 us
    unnamed x2, other arithmetic  16 us
    psum x1, waiting for transfers between devices, body(): lax.psum(normed_part.astype(jnp.bfloat16), 'tensor').astype(jnp.float32)  15.2 us
    all_to_all x1, starting transfers between devices, body(): lax.all_to_all(mixed_cot, 'tm', split_axis=1, concat_axis=0, tiled=True)  7.8 us
  transfers between devices with their start and end apart: 10, of which 8 were waited for; matrix products, arithmetic and copies ran while one was open for 20% of the time, Pallas kernels for 0%

profile of v1, /device:TPU:0, one launch (start us, length us, event | category | flops | bytes accessed | tf_op | source)
XLA Modules:
  0.0 358.1 jit_solution(14929947686857915444)
XLA Ops:
  8.0 2.2 fusion.29
  10.2 0.8 copy.115
  11.6 4.9 %reduce.4 = bf16[1024,192]{1,0:T(8,128)(2,1)} reduce(bf16[1024,1,192]{2,1,0:T(2,128)(2,1)S(1)} %bitcast.147, bf16[]{:T(256)} %broadcast.97), dimensions={1}, to_apply=%bitcast.110.reduce_sub_computation | reduce | bytes 786434
  16.5 2.4 reshape.160
  18.9 7.8 %all-to-all-start.2 = ((bf16[8,2,12288]{2,1,0:T(2,128)(2,1)}), bf16[8,2,12288]{2,1,0:T(2,128)(2,1)S(1)}, u32[]{:S(2)}, u32[]{:S(2)}) async-start(bf16[8,2,12288]{2,1,0:T(2,128)(2,1)} %reshape.160), calls=%async_computation.2 | async-start | bytes 786432 | tf_op jit(solution)/shard_map/all_to_all | solution.py:106
  27.7 2.3 fusion.17
  30.0 6.2 %copy.106 = bf16[1,1024,576]{2,0,1:T(2,128)(2,1)} copy(bf16[1,1024,576]{1,2,0:T(8,128)(2,1)} %fusion.17) | data formatting | bytes 2359296 | tf_op jit(solution)/shard_map/reshape | solution.py:53
  36.2 11.0 %reduce.5 = bf16[1024,576]{1,0:T(8,128)(2,1)} reduce(bf16[1024,1,576]{2,1,0:T(2,128)(2,1)} %bitcast.141, bf16[]{:T(256)} %broadcast.97), dimensions={1}, to_apply=%bitcast.108.reduce_sub_computation | reduce | bytes 2359298
  47.2 4.4 %reshape.158 = bf16[8,2,36864]{2,1,0:T(2,128)(2,1)} reshape(bf16[1024,576]{1,0:T(8,128)(2,1)} %reduce.5) | data formatting | bytes 2359296
  51.6 6.2 %all-to-all-start = ((bf16[8,2,36864]{2,1,0:T(2,128)(2,1)}), bf16[8,2,36864]{2,1,0:T(2,128)(2,1)}, u32[]{:S(2)}, u32[]{:S(2)}) async-start(bf16[8,2,36864]{2,1,0:T(2,128)(2,1)} %reshape.158), calls=%async_computation | async-start | bytes 2359296 | tf_op jit(solution)/shard_map/all_to_all | solution.py:87
  58.2 2.4 reshape.161
  60.6 1.7 copy.116
  62.3 1.8 copy.143
  64.1 22.0 %all-to-all-done = bf16[8,2,36864]{2,1,0:T(2,128)(2,1)} async-done(((bf16[8,2,36864]{2,1,0:T(2,128)(2,1)}), bf16[8,2,36864]{2,1,0:T(2,128)(2,1)}, u32[]{:S(2)}, u32[]{:S(2)}) %all-to-all-start) | async-done | bytes 1179680 | tf_op jit(solution)/shard_map/all_to_all | solution.py:87
  86.1 6.5 %reshape.159 = bf16[1024,1,576]{2,1,0:T(2,128)(2,1)} reshape(bf16[8,2,36864]{2,1,0:T(2,128)(2,1)} %all-to-all-done) | data formatting | bytes 2359296
  92.6 6.0 %copy.107 = bf16[1,1024,576]{1,2,0:T(8,128)(2,1)} copy(bf16[1,1024,576]{2,0,1:T(2,128)(2,1)} %bitcast.142) | data formatting | bytes 2359296 | tf_op jit(solution)/shard_map/all_to_all | solution.py:87
  98.6 1.6 copy.142
  100.2 1.0 fusion.60
  101.2 1.6 copy.138
  102.8 2.5 copy.137
  105.3 2.4 copy.139
  107.7 2.0 fusion.62
  109.7 0.7 fusion.32
  110.4 0.8 multiply_divide_fusion
  111.4 1.6 fusion.39
  113.0 2.3 copy.113
  115.3 2.2 fusion.41
  117.5 2.2 copy.118
  119.8 2.4 fusion.20
  122.5 1.9 convert_reduce_fusion.1
  124.5 1.0 fusion.58
  125.6 1.0 fusion.22
  127.2 2.0 pad_add_fusion
  129.2 4.2 %copy.121 = bf16[8,128,3,3,64]{1,4,3,2,0:T(8,128)(2,1)} copy(bf16[8,128,3,3,64]{4,0,3,1,2:T(8,128)(2,1)} %pad_add_fusion) | data formatting | bytes 2359296 | tf_op jit(solution)/shard_map/transpose(jvp())/add_any | solution.py:33
  133.4 32.7 %all_to_all.16 = bf16[8,128,576]{1,2,0:T(8,128)(2,1)} all-to-all(bf16[8,128,576]{1,2,0:T(8,128)(2,1)} %bitcast.144), channel_id=1, replica_groups=mesh['tm'=8,'tensor'=4] {'tm'}, dimensions={0} | all-to-all | bytes 2359296 | tf_op jit(solution)/shard_map/all_to_all | solution.py:110
  166.1 3.5 all-to-all-start.1
  169.6 3.8 %fusion.16 = bf16[1,1024,768]{2,1,0:T(8,128)(2,1)} fusion(bf16[768,576]{0,1:T(8,128)(2,1)S(1)} %bitcast.139, bf16[8,128,576]{1,2,0:T(8,128)(2,1)} %all_to_all.16), kind=kOutput, calls=%fused_computation.31 | convolution fusion | flops 906756096 | bytes 3637248 | tf_op jit(solution)/shard_map/dot_general | solution.py:67
  173.5 7.0 %all-to-all-done.1 = bf16[8,128,192]{1,2,0:T(8,128)(2,1)S(1)} async-done(((bf16[8,128,192]{1,2,0:T(8,128)(2,1)}), bf16[8,128,192]{1,2,0:T(8,128)(2,1)S(1)}, u32[]{:S(2)}, u32[]{:S(2)}) %all-to-all-start.1) | async-done | bytes 393248 | tf_op jit(solution)/shard_map/all_to_all | solution.py:93
  180.6 3.0 fusion.23
  183.7 1.8 fusion.15
  185.5 8.4 %copy.130 = bf16[1,1024,768]{1,0,2:T(2,128)(2,1)} copy(bf16[1,1024,768]{2,1,0:T(8,128)(2,1)} %fusion.15) | data formatting | bytes 3145728
  193.9 3.7 %copy.158 = bf16[768,1,1024]{2,0,1:T(8,128)(2,1)} copy(bf16[768,1,1024]{2,1,0:T(2,128)(2,1)} %bitcast.140) | data formatting | bytes 3145728
  197.7 1.4 copy_bitcast_fusion.1
  199.2 3.3 fusion.4
  202.5 15.2 %all-reduce.5.cloned.1.call-done = bf16[1,1024,768]{2,1,0:T(8,128)(2,1)} async-done(((bf16[1,1024,768]{2,1,0:T(8,128)(2,1)}), bf16[1,1024,768]{2,1,0:T(8,128)(2,1)}) %all-reduce.5.cloned.1.call-update) | async-done | bytes 1572880 | tf_op jit(solution)/shard_map/psum | solution.py:113
  217.7 1.8 convert_element_type.118
  219.6 1.2 multiply_reduce_fusion.2
  220.8 2.4 multiply_reduce_fusion.3
  223.2 1.5 collective-permute-start
  224.8 2.1 collective-permute-done
  226.9 1.5 collective-permute-start.1
  228.3 2.1 collective-permute-done.1
  230.4 2.4 collective-permute-start.2
  232.8 1.9 convert_element_type.92
  234.7 11.4 %reduce-scatter.12.cloned.1.call-done = f32[96,192]{1,0:T(8,128)} async-done(((f32[768,192]{1,0:T(8,128)}), f32[96,192]{1,0:T(8,128)}) %reduce-scatter.12.cloned.1.call-update) | async-done | bytes 73744
  246.1 1.6 copy.133
  247.7 0.9 copy.125
  249.2 26.3 %reduce-scatter.10.cloned.1.call-done = bf16[192,1024]{1,0:T(8,128)(2,1)} async-done(((bf16[768,1024]{1,0:T(8,128)(2,1)}), bf16[192,1024]{1,0:T(8,128)(2,1)}) %reduce-scatter.10.cloned.1.call-update) | async-done | bytes 393232
  275.5 1.4 reshape_bitcast_fusion
  276.9 1.1 copy.131
  278.0 1.8 add_convert_fusion.1
  279.8 0.9 copy.124
  280.7 67.9 %reduce-scatter.8.cloned.1.call-done = f32[96,3,192]{2,0,1:T(8,128)} async-done(((f32[768,3,192]{2,0,1:T(8,128)}), f32[96,3,192]{2,0,1:T(8,128)}) %reduce-scatter.8.cloned.1.call-update) | async-done | bytes 221200 | tf_op jit(solution)/shard_map/reduce_scatter | solution.py:126
  348.6 1.6 convert_element_type.120
  (62 shorter events, 4.2 us)
Async XLA Ops:
  8.0 19.7 %copy-start = (bf16[768,3,192]{0,2,1:T(8,128)(2,1)S(1)}, bf16[768,3,192]{0,2,1:T(8,128)(2,1)}, u32[]{:S(2)}) copy-start(bf16[768,3,192]{0,2,1:T(8,128)(2,1)} %param.8) | copy-start | bytes 2654212
  11.6 15.2 %copy-start.1 = (bf16[1,1024,768]{2,1,0:T(8,128)(2,1)S(1)}, bf16[1,1024,768]{2,1,0:T(8,128)(2,1)}, u32[]{:S(2)}) copy-start(bf16[1,1024,768]{2,1,0:T(8,128)(2,1)} %param.6) | copy-start | bytes 4718596
  18.9 32.7 %all-to-all-start.2 = ((bf16[8,2,12288]{2,1,0:T(2,128)(2,1)}), bf16[8,2,12288]{2,1,0:T(2,128)(2,1)S(1)}, u32[]{:S(2)}, u32[]{:S(2)}) async-start(bf16[8,2,12288]{2,1,0:T(2,128)(2,1)} %reshape.160), calls=%async_computation.2 | async-start | bytes 786432 | tf_op jit(solution)/shard_map/all_to_all | solution.py:106
  26.7 0.9 copy-start.15
  51.6 6.3 %copy-start.14 = (s32[8,16,2]{1,2,0:T(2,128)S(1)}, s32[8,16,2]{1,2,0:T(2,128)}, u32[]{:S(2)}) copy-start(s32[8,16,2]{1,2,0:T(2,128)} %param.10) | copy-start | bytes 3076
  51.6 6.6 %copy-start.8 = (bf16[8,2,12288]{2,1,0:T(2,128)(2,1)}, bf16[8,2,12288]{2,1,0:T(2,128)(2,1)S(1)}, u32[]{:S(2)}) copy-start(bf16[8,2,12288]{2,1,0:T(2,128)(2,1)S(1)} %all-to-all-done.2) | copy-start | bytes 1179652
  51.6 34.5 %all-to-all-start = ((bf16[8,2,36864]{2,1,0:T(2,128)(2,1)}), bf16[8,2,36864]{2,1,0:T(2,128)(2,1)}, u32[]{:S(2)}, u32[]{:S(2)}) async-start(bf16[8,2,36864]{2,1,0:T(2,128)(2,1)} %reshape.158), calls=%async_computation | async-start | bytes 2359296 | tf_op jit(solution)/shard_map/all_to_all | solution.py:87
  109.7 1.5 copy-start.2
  109.7 1.5 copy-start.6
  109.7 1.7 copy-start.10
  119.7 2.4 copy-start.3
  119.7 2.4 copy-start.7
  119.7 2.5 copy-start.11
  119.7 2.7 copy-start.12
  119.7 2.8 copy-start.13
  124.4 1.1 copy-start.5
  166.1 14.5 %all-to-all-start.1 = ((bf16[8,128,192]{1,2,0:T(8,128)(2,1)}), bf16[8,128,192]{1,2,0:T(8,128)(2,1)S(1)}, u32[]{:S(2)}, u32[]{:S(2)}) async-start(bf16[8,128,192]{1,2,0:T(8,128)(2,1)} %bitcast.10), calls=%async_computation.1 | async-start | bytes 786432 | tf_op jit(solution)/shard_map/all_to_all | solution.py:93
  169.5 48.2 %all-reduce.5.cloned.1.call-start = ((), (), s32[]{:S(2)}) async-start(), calls=%async_computation.7 | async-start | bytes 3145728 | tf_op jit(solution)/shard_map/psum | solution.py:113
  173.4 10.2 %copy-start.9 = (bf16[192,768]{1,0:T(8,128)(2,1)S(1)}, bf16[192,768]{1,0:T(8,128)(2,1)}, u32[]{:S(2)}) copy-start(bf16[192,768]{1,0:T(8,128)(2,1)} %param.9) | copy-start | bytes 884740
  173.5 72.7 %reduce-scatter.12.cloned.1.call-start = ((), (), s32[]{:S(2)}) async-start(), calls=%async_computation.10 | async-start | bytes 884736
  183.6 91.9 %reduce-scatter.10.cloned.1.call-start = ((), (), s32[]{:S(2)}) async-start(), calls=%async_computation.9 | async-start | bytes 1966080
  197.7 151.0 %reduce-scatter.8.cloned.1.call-start = ((), (), s32[]{:S(2)}) async-start(), calls=%async_computation.8 | async-start | bytes 2654208 | tf_op jit(solution)/shard_map/reduce_scatter | solution.py:126
  217.7 1.9 copy-start.4
  223.2 3.6 %collective-permute-start = (f32[192]{0:T(256)S(1)}, f32[192]{0:T(256)S(1)}, u32[]{:S(2)}, u32[]{:S(2)}) collective-permute-start(f32[192]{0:T(256)S(1)} %get-tuple-element.46), channel_id=1, source_target_pairs={{0,4},{4,0},{8,12},{12,8},{16,20},{20,16},{24,28},{28,24},{1,5},{5... | collective-permute-start | bytes 2312 | tf_op jit(solution)/shard_map/ppermute | solution.py:132
  226.9 3.6 collective-permute-start.1
  230.4 18.2 %collective-permute-start.2 = (f32[192]{0:T(256)S(1)}, f32[192]{0:T(256)S(1)}, u32[]{:S(2)}, u32[]{:S(2)}) collective-permute-start(f32[192]{0:T(256)S(1)} %add.69), channel_id=1, source_target_pairs={{0,16},{4,20},{8,24},{12,28},{16,0},{20,4},{24,8},{28,12},{1,17},{... | collective-permute-start | bytes 2312 | tf_op jit(solution)/shard_map/ppermute | solution.py:132
Sparse Core Ops, SparseCore 0:
  173.6 44.1 all-reduce.4
Sparse Core Ops, SparseCore 1:
  183.7 62.4 reduce-scatter.11
  248.5 26.9 reduce-scatter.9
  278.8 69.7 reduce-scatter.7
